TPU v7x, 128 devices: a whole 4x4x4 slice. The times are simulated.
128 devices in a mesh: freq: 8 (over x, core), tile: 16 (over z, y).
Axes of the slice: x: 4, y: 4, z: 4, core: 2. Of those that a mesh axis runs over, the one named last changes fastest.
Arguments:
- virtual_source_trace: bfloat16 [512, 4, 8400], P(('freq', 'tile')), may hold values from -6 to 6
- v_bases: bfloat16 [8, 192, 120, 2, 32, 70], P('freq', 'tile'), may hold values from -0.75 to 0.75
- u_bases: bfloat16 [8, 192, 120, 2, 32, 70], P('freq', 'tile'), may hold values from -0.09375 to 0.09375
- ranks: int32 [8, 192, 120], P('freq', 'tile'), may hold values from 16 to 32, as said below
- freq_bin: int32 [8], replicated, may hold values from 1 to 255
- slab_order: int32 [128], replicated, may hold values from 0 to 127, each once
Outputs:
- redatumed: bfloat16 [512, 4, 13440], P(('freq', 'tile'))
Inputs may be any that keep to these rules, and one draw needn't show every extreme that they name: `ranks`: every rank is 16 or 32.
All inputs are finite; a program needn't handle non-finite values.
Results may differ from a plain program's by a relative error of at most 0.008.
Values may be sent and summed in bfloat16 or wider, within the bound.
A program may use at most 192 MiB of HBM per device.

v0:
```python
import math

import jax
import jax.numpy as jnp
from jax import lax
from jax.sharding import PartitionSpec as P


def angles_of(freq_bin, times, total):
    products = freq_bin[:, None] * times[None, :] % total
    return products.astype(jnp.float32) * (2.0 * math.pi / total)


def apply_kernel(v_part, u_part, rank_part, frequency_spectra):
    width = v_part.shape[3]
    projected = jnp.einsum(
        "ijcrp,dvjp->ijcdrv", v_part, frequency_spectra, preferred_element_type=jnp.float32
    )
    coef_re = projected[:, :, 0, 0] - projected[:, :, 1, 1]
    coef_im = projected[:, :, 0, 1] + projected[:, :, 1, 0]
    rank_mask = (jnp.arange(width, dtype=jnp.int32)[None, None, :] < rank_part[:, :, None]).astype(
        jnp.float32
    )[..., None]
    coefs = jnp.stack([coef_re * rank_mask, coef_im * rank_mask], axis=2).astype(jnp.bfloat16)
    rows_dev = v_part.shape[0] * v_part.shape[4]
    expanded = jnp.einsum("ijcrq,ijdrm->cdmiq", u_part, coefs, preferred_element_type=jnp.float32)
    out_re = (expanded[0, 0] - expanded[1, 1]).reshape(coefs.shape[4], rows_dev)
    out_im = (expanded[0, 1] + expanded[1, 0]).reshape(coefs.shape[4], rows_dev)
    return jnp.stack([out_re, out_im])


def local(virtual_source_trace, v_bases, u_bases, ranks, freq_bin, slab_order):
    n_tile = lax.axis_size("tile")
    n_freq = lax.axis_size("freq")
    steps_dev = virtual_source_trace.shape[0]
    sources = virtual_source_trace.shape[1]
    total = steps_dev * n_freq * n_tile
    count_freq = freq_bin.shape[0]
    device = lax.axis_index("freq") * n_tile + lax.axis_index("tile")
    first = lax.dynamic_index_in_dim(slab_order, device, 0, keepdims=False) * steps_dev
    times = first + jnp.arange(steps_dev, dtype=jnp.int32)
    angles = angles_of(freq_bin, times, total)
    forward = jnp.stack([jnp.cos(angles), -jnp.sin(angles)], axis=1) / math.sqrt(total)
    signal = virtual_source_trace.astype(jnp.float32)
    partial_value = jnp.einsum("fct,tvs->fcvs", forward, signal, precision=lax.Precision.HIGHEST)
    grouped = lax.psum_scatter(partial_value, "freq", scatter_dimension=0, tiled=True)
    frequency_spectra = lax.psum(grouped, "tile").astype(jnp.bfloat16)
    columns = v_bases.shape[2]
    tile_width = v_bases.shape[5]
    frequency_spectra = frequency_spectra.reshape(2, sources, columns, tile_width)
    received = apply_kernel(v_bases[0], u_bases[0], ranks[0], frequency_spectra)
    piece = received[None]
    gathered = lax.all_gather(piece, ("freq", "tile"), axis=0, tiled=True)
    gathered = gathered.reshape(n_freq, n_tile, 2, sources, -1)
    inverse = jnp.stack([jnp.cos(angles.T), -jnp.sin(angles.T)], axis=2) / math.sqrt(count_freq)
    redatumed = jnp.einsum("tgc,gkcvn->tvkn", inverse, gathered, precision=lax.Precision.HIGHEST)
    return redatumed.reshape(steps_dev, sources, -1).astype(jnp.bfloat16)


def solution(mesh):
    in_specs = (
        P(("freq", "tile"), None, None),
        P("freq", "tile", None, None, None, None),
        P("freq", "tile", None, None, None, None),
        P("freq", "tile", None),
        P(),
        P(),
    )
    out_specs = P(("freq", "tile"), None, None)
    return jax.shard_map(local, mesh=mesh, in_specs=in_specs, out_specs=out_specs, check_vma=False)
```

profile of v0, /device:TPU:1, one launch (start us, length us, event | category | flops | bytes accessed | tf_op | source)
XLA Modules:
  0.0 297.1 jit_solution(16742944075265541765)
XLA Ops:
  6.5 1.2 dynamic_slice.4
  8.4 0.8 fusion.45
  9.2 2.0 fusion.24
  11.2 2.2 copy.43
  13.5 39.3 %copy.57 = bf16[12,120,2,32,70,1]{4,3,2,0,5,1:T(8,128)(2,1)} copy(bf16[12,120,2,32,70,1]{1,3,4,2,0,5:T(8,128)(2,1)} %bitcast.72) | data formatting | bytes 25804800 | tf_op jit(solution)/shard_map/squeeze | solution.py:51
  52.9 0.1 copy.67
  53.0 0.6 dynamic-slice
  53.6 0.3 fusion.23
  53.9 27.0 %all-reduce.4.cloned.1.call-done = f32[8,2,4,8400]{3,2,1,0:T(4,128)} async-done(((f32[8,2,4,8400]{3,2,1,0:T(4,128)}), f32[8,2,4,8400]{3,2,1,0:T(4,128)}) %all-reduce.4.cloned.1.call-update) | async-done | bytes 2150416
  80.9 1.6 constant_dynamic-slice_fusion
  82.5 64.3 %all-reduce.5 = bf16[1,2,4,8400]{3,2,1,0:T(4,128)(2,1)S(1)} all-reduce(f32[1,2,4,8400]{3,2,1,0:T(4,128)S(1)} %constant_dynamic-slice_fusion), channel_id=1, replica_groups=mesh['freq'=8,'tile'=16] {'tile'}, use_global_device_ids=true, to_apply=%region_1.2 | all-reduce | flops 67200 | bytes 403200 | tf_op jit(solution)/shard_map/psum | solution.py:47
  146.8 0.3 reshape.343
  147.1 35.9 %convolution_bitcast_fusion = f32[12,120,2,2,32,4]{4,5,2,0,3,1:T(4,128)} fusion(bf16[12,120,2,32,70,1]{4,3,2,0,5,1:T(8,128)(2,1)} %copy.57, bf16[2,4,120,70,1,1]{3,2,1,0,5,4:T(8,128)(2,1)S(1)} %bitcast.74), kind=kOutput, calls=%fused_computation.2 | convolution fusion | flops 103219200 | bytes 15985920 | tf_op jit(solution)/shard_map/ijcrp,dvjp->ijcdrv/dot_general | solution.py:16
  183.0 5.4 %fusion.10 = (bf16[12,120,1,32,4]{3,4,0,1,2:T(4,128)(2,1)S(1)}, bf16[12,120,1,32,4]{3,4,0,1,2:T(4,128)(2,1)S(1)}) fusion(f32[12,120,2,2,32,4]{4,5,2,0,3,1:T(4,128)} %convolution_bitcast_fusion, f32[12,120,32]{2,0,1:T(8,128)S(1)} %fusion.23), kind=kLoop, calls=%fused_computation.13 | loop fusion | flops 1105920 | bytes 3870720 | tf_op jit(solution)/shard_map/convert
  188.4 2.5 maximum_bitcast_fusion
  190.9 3.4 %copy.58 = bf16[12,120,2,32,4,1]{1,4,3,5,2,0:T(4,128)(2,1)} copy(bf16[12,120,2,32,4,1]{3,4,0,1,2,5:T(4,128)(2,1)S(1)} %maximum_bitcast_fusion) | data formatting | bytes 1474560 | tf_op jit(solution)/shard_map/stack | solution.py:24
  194.2 10.7 %fusion.20 = f32[2,2,4,12,70]{4,2,0,1,3:T(4,128)S(1)} fusion(bf16[12,120,2,32,4,1]{1,4,3,5,2,0:T(4,128)(2,1)} %copy.58, bf16[12,120,2,32,70,1]{1,3,4,2,0,5:T(8,128)(2,1)} %bitcast.76), kind=kOutput, calls=%fused_computation.19 | convolution fusion | flops 103219200 | bytes 13693440 | tf_op jit(solution)/shard_map/ijcrq,ijdrm->cdmiq/dot_general | solution.py:26
  205.0 0.1 add.86
  205.1 0.1 sub.29
  205.2 0.6 pad_maximum_fusion
  205.8 0.1 fusion.44
  206.0 76.9 %all-gather.3.cloned.1.call-done = f32[256,4,840]{2,1,0:T(4,128)} async-done(((f32[2,4,840]{2,1,0:T(4,128)}), f32[256,4,840]{2,1,0:T(4,128)}) %all-gather.3.cloned.1.call-update) | async-done | bytes 3440656 | tf_op jit(solution)/shard_map/all_gather | solution.py:53
  282.8 5.9 %fusion.17 = bf16[4,4,16,840]{3,0,1,2:T(4,128)(2,1)S(1)} fusion(f32[8,16,2,4,840]{4,3,2,1,0:T(4,128)} %bitcast.73, f32[4,8,1]{1,0,2:T(4,128)S(1)} %get-tuple-element.10, f32[4,8,1]{1,0,2:T(4,128)S(1)} %get-tuple-element.9), kind=kOutput, calls=%fused_computation.18 | convolution fusion | flops 41502848 | bytes 3870976 | tf_op jit(solution)/shard_map/tgc,gkcvn->tvkn/dot_general | solution.py:56
  288.8 1.4 convert_element_type.55
  (15 shorter events, 0.2 us)
Async XLA Ops:
  6.5 74.3 %all-reduce.4.cloned.1.call-start = ((), (), s32[]{:S(2)}) async-start(), calls=%async_computation.1 | async-start | bytes 4325376
  13.5 269.4 %all-gather.3.cloned.1.call-start = ((), (), s32[]{:S(2)}) async-start(), calls=%async_computation | async-start | bytes 3698688 | tf_op jit(solution)/shard_map/all_gather | solution.py:53
  13.5 39.3 %copy-start = (s32[1,12,120]{2,0,1:T(1,128)S(1)}, s32[1,12,120]{2,0,1:T(1,128)}, u32[]{:S(2)}) copy-start(s32[1,12,120]{2,0,1:T(1,128)} %param.9) | copy-start | bytes 17284
  13.5 39.4 %copy-start.2 = (u32[128]{0:T(128)S(1)}, u32[128]{0:T(128)}, u32[]{:S(2)}) copy-start(u32[128]{0:T(128)} %constant.50) | copy-start | bytes 1540
  194.2 11.6 %copy-start.1 = (s32[8]{0:T(128)S(1)}, s32[8]{0:T(128)}, u32[]{:S(2)}) copy-start(s32[8]{0:T(128)} %param.10) | copy-start | bytes 100
Sparse Core Ops, SparseCore 0:
  13.6 67.2 all-reduce.3
  205.9 76.8 all-gather.2
where the time goes:
time: 297 us
  waiting for transfers between devices  104 us (35%)
  blocking collectives  64.3 us (22%)
  matrix products  54.6 us (18%)
  local copies, waits for them, and re-layouts  50.4 us (17%)
  between operations  14.2 us (5%)
  other arithmetic  9.72 us (3%)
    all_gather x1, waiting for transfers between devices, local(): gathered = lax.all_gather(piece, ('freq', 'tile'), axis=0, tiled=True)  76.9 us
    psum x1, blocking collectives, local(): frequency_spectra = lax.psum(grouped, 'tile').astype(jnp.bfloat16)  64.3 us
    squeeze x1, local copies, waits for them, and re-layouts, local(): received = apply_kernel(v_bases[0], u_bases[0], ranks[0], frequency_spectra)  39.3 us
    dot_general x1, matrix products, apply_kernel(): jnp.einsum('ijcrp,dvjp->ijcdrv', v_part, frequency_spectra, preferred_ele...  35.9 us
    unnamed x3, waiting for transfers between devices  27 us
    dot_general x1, matrix products, apply_kernel(): jnp.einsum('ijcrq,ijdrm->cdmiq', u_part, coefs, preferred_element_type=jn...  10.7 us
  transfers between devices with their start and end apart: 2, of which 2 were waited for; matrix products, arithmetic and copies ran while one was open for 14% of the time, Pallas kernels for 0%

commit v1 on v0

v1 whole, which is shorter than its diff:
```python
import functools
import math

import jax
import jax.numpy as jnp
from jax import lax
from jax.experimental import pallas as pl
from jax.experimental.pallas import tpu as pltpu
from jax.sharding import PartitionSpec as P

F32, BF16 = jnp.float32, jnp.bfloat16
MESH = pl.DeviceIdType.MESH
EXT = 70
COLS = 120
RANK = 32
NV = 4
NT = 4
ROWS = 12
NTILE = 16
NFREQ = 8
CHUNK = 5
OUT = 13440
NT_DIMS = (((1,), (1,)), ((), ()))


def chunk_start(k):
    return (k * (EXT - CHUNK) + 7) // (NTILE - 1)


def split(x):
    hi = x.astype(BF16)
    return hi, (x - hi.astype(F32)).astype(BF16)


def tree(xs):
    while len(xs) > 1:
        xs = [a + b for a, b in zip(xs[::2], xs[1::2])] + ([xs[-1]] if len(xs) % 2 else [])
    return xs[0]


def peers():
    g, k = lax.axis_index("freq"), lax.axis_index("tile")
    over_tile = [(d, lax.rem(k + d, NTILE)) for d in range(1, NTILE)]
    over_freq = [(d, lax.rem(g + d, NFREQ)) for d in range(1, NFREQ)]
    return g, k, over_tile, over_freq


def enter(over_tile, over_freq):
    barrier = pltpu.get_barrier_semaphore()
    for _, kk in over_tile:
        pl.semaphore_signal(barrier, inc=1, device_id={"tile": kk}, device_id_type=MESH)
    for _, f in over_freq:
        pl.semaphore_signal(barrier, inc=1, device_id={"freq": f}, device_id_type=MESH)
    pl.semaphore_wait(barrier, NTILE + NFREQ - 2)


def remote(src, dst, send, recv, axis, to):
    return pltpu.make_async_remote_copy(
        src_ref=src, dst_ref=dst, send_sem=send, recv_sem=recv, device_id={axis: to}, device_id_type=MESH
    )


def spectra_kernel(t_ref, w_ref, x_ref, a1, s2, b2, s3, b3, own, ss1, rs1, ss2, rs2, ss3, rs3):
    g, k, over_tile, over_freq = peers()
    enter(over_tile, over_freq)
    mine = pltpu.make_async_copy(t_ref.at[pl.ds(chunk_start(k), CHUNK)], a1.at[k], own)
    mine.start()
    sends = []
    for _, kk in over_tile:
        c = remote(t_ref.at[pl.ds(chunk_start(kk), CHUNK)], a1.at[k], ss1.at[kk], rs1.at[k], "tile", kk)
        c.start()
        sends.append(c)
    mine.wait()
    for _, kk in over_tile:
        remote(t_ref.at[pl.ds(0, CHUNK)], a1.at[kk], ss1.at[kk], rs1.at[kk], "tile", kk).wait_recv()
    for p in range(CHUNK):
        data = a1[:, p].reshape(NTILE * 16, 128)
        both = jnp.dot(w_ref[...], data, preferred_element_type=F32)
        s2[:, p] = (both[:64] + both[64:]).reshape(NFREQ, 8, 128).astype(BF16)
    for _, f in over_freq:
        c = remote(s2.at[f], b2.at[g], ss2.at[f], rs2.at[g], "freq", f)
        c.start()
        sends.append(c)
    total = s2[g].astype(F32)
    for _, f in over_freq:
        remote(s2.at[f], b2.at[f], ss2.at[f], rs2.at[f], "freq", f).wait_recv()
        total = total + b2[f].astype(F32)
    s3[...] = total.astype(BF16)
    for _, kk in over_tile:
        c = remote(s3, b3.at[k], ss3.at[kk], rs3.at[k], "tile", kk)
        c.start()
        sends.append(c)
    b3[k] = s3[...]
    for _, kk in over_tile:
        remote(s3, b3.at[kk], ss3.at[kk], rs3.at[kk], "tile", kk).wait_recv()
    for kk in range(NTILE):
        for p in range(CHUNK):
            x = b3[kk, p].astype(F32)
            xr, xi = x[0:4], x[4:8]
            x_ref[chunk_start(kk) + p] = jnp.concatenate([xr, xi - xr, xr + xi, xr], axis=0)
    for c in sends:
        c.wait_send()


def spectra(t, w):
    vmem = pl.BlockSpec(memory_space=pltpu.VMEM)
    dma = pltpu.SemaphoreType.DMA
    return pl.pallas_call(
        spectra_kernel,
        out_shape=jax.ShapeDtypeStruct((EXT, 16, 128), F32),
        in_specs=[vmem, vmem],
        out_specs=vmem,
        scratch_shapes=[
            pltpu.VMEM((NTILE, CHUNK, 16, 128), BF16),
            pltpu.VMEM((NFREQ, CHUNK, 8, 128), BF16),
            pltpu.VMEM((NFREQ, CHUNK, 8, 128), BF16),
            pltpu.VMEM((CHUNK, 8, 128), BF16),
            pltpu.VMEM((NTILE, CHUNK, 8, 128), BF16),
            dma,
            dma((NTILE,)), dma((NTILE,)), dma((NFREQ,)), dma((NFREQ,)), dma((NTILE,)), dma((NTILE,)),
        ],
        compiler_params=pltpu.CompilerParams(collective_id=0, has_side_effects=True),
    )(t, w)


def project(v_ref, x_ref, rank_row, ct):
    row = lax.broadcasted_iota(jnp.int32, (8, COLS), 0)
    for h in range(2):
        def body(p, acc):
            acc = list(acc)
            for a in range(2):
                r = 16 * h + 8 * a
                re = v_ref[0, 0, p, r:r + 8, :].astype(F32)
                im = v_ref[0, 1, p, r:r + 8, :].astype(F32)
                for n, b in enumerate((re + im, re, im)):
                    for v in range(NV):
                        m = 4 * n + v
                        acc[12 * a + m] += b * jnp.broadcast_to(x_ref[p, m:m + 1, :COLS], (8, COLS))
            return tuple(acc)

        acc = lax.fori_loop(0, EXT, body, (jnp.zeros((8, COLS), F32),) * 24, unroll=5)
        for a in range(2):
            keep = row + (16 * h + 8 * a) < rank_row
            for v in range(NV):
                k1, k2, k3 = (acc[12 * a + 4 * n + v] for n in range(3))
                re = jnp.where(keep, k1 - k3, 0.0).astype(BF16)
                im = jnp.where(keep, k1 + k2, 0.0).astype(BF16)
                n = 64 * a + 16 * v
                ct[h, n:n + 8, 0:COLS] = re
                ct[h, n:n + 8, 128:128 + COLS] = -im
                ct[h, n + 8:n + 16, 0:COLS] = im
                ct[h, n + 8:n + 16, 128:128 + COLS] = re


def expand(u_ref, ct, diag, step):
    lane = lax.broadcasted_iota(jnp.int32, (step * 16, 128), 1)
    low = lax.broadcasted_iota(jnp.int32, (step, 8, 128), 2) < 64
    for h in range(2):
        @pl.loop(0, EXT // step)
        def _(s):
            us = []
            for c in range(2):
                u = u_ref[0, c, pl.ds(s * step, step), 16 * h:16 * h + 16, :].reshape(step * 16, 128)
                us.append(jnp.where(lane < COLS, u, jnp.zeros_like(u)))
            z = lax.dot_general(jnp.concatenate(us, axis=1), ct[h], NT_DIMS, preferred_element_type=F32)
            z = z.reshape(step, 2, 8, 128)
            diag[h, pl.ds(s * step * 8, step * 8), :] = jnp.where(low, z[:, 0], z[:, 1]).reshape(step * 8, 128)


def collect(diag):
    lane = lax.broadcasted_iota(jnp.int32, (EXT, 128), 1) % 8
    halves = []
    for h in range(2):
        tot = diag[h, pl.ds(0, EXT, stride=8), :]
        for b in range(1, 8):
            tot = jnp.where(lane == b, diag[h, pl.ds(b, EXT, stride=8), :], tot)
        halves.append(tot)
    hi, lo = split(jnp.concatenate(halves, axis=1))
    rows = lax.broadcasted_iota(jnp.int32, (8, 256), 0)
    lanes = lax.broadcasted_iota(jnp.int32, (8, 256), 1)
    pick = ((lanes % 64) // 8 == (rows % 4) * 2 + rows // 4).astype(BF16)
    dot = functools.partial(lax.dot_general, dimension_numbers=NT_DIMS, preferred_element_type=F32)
    return dot(pick, hi) + dot(pick, lo)


def apply_kernel(step, rank_ref, x_ref, v_ref, u_ref, out_ref, ct, diag):
    @pl.when(pl.program_id(0) == 0)
    def _():
        ct[...] = jnp.zeros_like(ct)

    project(v_ref, x_ref, rank_ref[0], ct)
    expand(u_ref, ct, diag, step)
    out_ref[0] = jnp.zeros((8, 128), F32)
    out_ref[0, :, 0:EXT] = collect(diag)


def apply(ranks, x, v, u, step=14):
    return pl.pallas_call(
        functools.partial(apply_kernel, step),
        grid=(ROWS,),
        out_shape=jax.ShapeDtypeStruct((ROWS, 8, 128), F32),
        in_specs=[
            pl.BlockSpec((1, 1, COLS), lambda i: (i, 0, 0)),
            pl.BlockSpec((EXT, 16, 128), lambda i: (0, 0, 0)),
            pl.BlockSpec((1, 2, EXT, RANK, COLS), lambda i: (i, 0, 0, 0, 0)),
            pl.BlockSpec((1, 2, EXT, RANK, 128), lambda i: (i, 0, 0, 0, 0)),
        ],
        out_specs=pl.BlockSpec((1, 8, 128), lambda i: (i, 0, 0)),
        scratch_shapes=[pltpu.VMEM((2, 128, 256), BF16), pltpu.VMEM((2, EXT * 8, 128), F32)],
    )(ranks, x, v, u)


def output_kernel(r_ref, w_ref, out_ref, s1, b1, s2, b2, ss1, rs1, ss2, rs2):
    g, k, over_tile, over_freq = peers()
    lane = lax.broadcasted_iota(jnp.int32, (8, 128), 1)
    zero = jnp.zeros((8, 128), F32)
    tiles = [zero] * 8
    for i in range(ROWS):
        a, off = divmod(EXT * i, 128)
        piece = pltpu.roll(r_ref[i], off, 1) if off else r_ref[i]
        tiles[a] = tiles[a] + jnp.where(lane >= off, piece, 0.0)
        if off + EXT > 128:
            tiles[a + 1] = tiles[a + 1] + jnp.where(lane < off, piece, 0.0)
    off = lax.rem(k * (EXT * ROWS), 128)
    rolled = [zero] + [pltpu.roll(t, off, 1) for t in tiles]
    for a in range(8):
        s1[:, 128 * a:128 * a + 128] = jnp.where(lane >= off, rolled[a + 1], rolled[a]).astype(BF16)
    enter(over_tile, over_freq)
    sends = []
    for _, f in over_freq:
        c = remote(s1, b1.at[g], ss1.at[f], rs1.at[g], "freq", f)
        c.start()
        sends.append(c)
    b1[g] = s1[...]
    for _, f in over_freq:
        remote(s1, b1.at[f], ss1.at[f], rs1.at[f], "freq", f).wait_recv()
    r = b1[...].reshape(64, 1024)
    both = jnp.concatenate([r, r], axis=0)
    for c in range(4):
        lanes = slice(256 * c, 256 * c + 256)
        res = jnp.dot(w_ref[...], both[:, lanes], preferred_element_type=F32)
        s2[:, :, lanes] = res.reshape(NTILE, 16, 256).astype(BF16)
    for _, kk in over_tile:
        c = remote(s2.at[kk], b2.at[k], ss2.at[kk], rs2.at[k], "tile", kk)
        c.start()
        sends.append(c)
    b2[k] = s2[k]
    for _, kk in over_tile:
        remote(s2.at[kk], b2.at[kk], ss2.at[kk], rs2.at[kk], "tile", kk).wait_recv()
    parts = [[] for _ in range(OUT // 128)]
    for kk in range(NTILE):
        a, off = divmod(kk * EXT * ROWS, 128)
        for t in range((off + EXT * ROWS + 127) // 128):
            parts[a + t].append((kk, t))
    for m, ps in enumerate(parts):
        vals = [b2[kk, :, 128 * t:128 * t + 128] for kk, t in ps]
        out_ref[:, 128 * m:128 * m + 128] = tree(vals)
    for c in sends:
        c.wait_send()


def output(r, w):
    vmem = pl.BlockSpec(memory_space=pltpu.VMEM)
    dma = pltpu.SemaphoreType.DMA
    return pl.pallas_call(
        output_kernel,
        out_shape=jax.ShapeDtypeStruct((16, OUT), BF16),
        in_specs=[vmem, vmem],
        out_specs=vmem,
        scratch_shapes=[
            pltpu.VMEM((8, 1024), BF16),
            pltpu.VMEM((NFREQ, 8, 1024), BF16),
            pltpu.VMEM((NTILE, 16, 1024), BF16),
            pltpu.VMEM((NTILE, 16, 1024), BF16),
            dma((NFREQ,)), dma((NFREQ,)), dma((NTILE,)), dma((NTILE,)),
        ],
        compiler_params=pltpu.CompilerParams(collective_id=1, has_side_effects=True),
    )(r, w)


def transforms(freq_bin, slab_order):
    g = lax.axis_index("freq")
    slabs = lax.dynamic_slice_in_dim(slab_order, g * NTILE, NTILE)
    times = (slabs[:, None] * NT + jnp.arange(NT, dtype=jnp.int32)[None, :]).reshape(-1)
    total = NT * NTILE * NFREQ
    angles = (freq_bin[:, None] * times[None, :] % total).astype(F32) * (2.0 * math.pi / total)
    trig = jnp.stack([jnp.cos(angles), -jnp.sin(angles)], axis=1)
    eye = jnp.eye(NV, dtype=F32)
    fwd = (trig[:, :, None, :, None] * eye[None, None, :, None, :]).reshape(64, 256) / math.sqrt(total)
    inv = (trig.transpose(2, 0, 1)[:, None, :, :, None] * eye[None, :, None, None, :]).reshape(256, 64)
    inv = inv / math.sqrt(NFREQ)
    return jnp.concatenate(split(fwd), axis=0), jnp.concatenate(split(inv), axis=1)


def local(virtual_source_trace, v_bases, u_bases, ranks, freq_bin, slab_order):
    fwd, inv = transforms(freq_bin, slab_order)
    t = virtual_source_trace.reshape(NT, NV, COLS, EXT).transpose(3, 0, 1, 2).reshape(EXT, 16, COLS)
    t = jnp.pad(t, ((0, 0), (0, 0), (0, 128 - COLS)))
    x = spectra(t, fwd)
    v = v_bases[0].transpose(0, 2, 4, 3, 1)
    u = u_bases[0].transpose(0, 2, 4, 3, 1)
    r = apply(ranks.reshape(ROWS, 1, COLS), x, v, u)
    return output(r, inv).reshape(NT, NV, OUT)


def solution(mesh):
    in_specs = (
        P(("freq", "tile"), None, None),
        P("freq", "tile", None, None, None, None),
        P("freq", "tile", None, None, None, None),
        P("freq", "tile", None),
        P(),
        P(),
    )
    out_specs = P(("freq", "tile"), None, None)
    return jax.shard_map(local, mesh=mesh, in_specs=in_specs, out_specs=out_specs, check_vma=False)
```

time: 297 us -> 97.6 us (0.33)
  waiting for transfers between devices: 104 us -> 0 us
  Pallas kernels: 0 us -> 86.3 us
  blocking collectives: 64.3 us -> 0 us
  matrix products: 54.6 us -> 0 us
  local copies, waits for them, and re-layouts: 50.4 us -> 7.35 us
  between operations: 14.2 us -> 0.1 us
  other arithmetic: 9.72 us -> 3.62 us
    pallas_call x0 -> x3, Pallas kernels: none -> 86.3 us  [the longest x1 42.5 us: apply(): pl.pallas_call(functools.partial(apply_kernel, step), grid=(ROWS,), out_s...]
    all_gather x1 -> x0, waiting for transfers between devices: 76.9 us -> none  [local(): gathered = lax.all_gather(piece, ('freq', 'tile'), axis=0, tiled=True)]
    psum x1 -> x0, blocking collectives: 64.3 us -> none  [local(): frequency_spectra = lax.psum(grouped, 'tile').astype(jnp.bfloat16)]
    dot_general x4 -> x0, matrix products: 54.6 us -> none  [the longest x1 35.9 us: apply_kernel(): jnp.einsum('ijcrp,dvjp->ijcdrv', v_part, frequency_spectra, preferred_ele...]
    squeeze x1 -> x0, local copies, waits for them, and re-layouts: 39.3 us -> none  [local(): received = apply_kernel(v_bases[0], u_bases[0], ranks[0], frequency_spectra)]
    unnamed x3 -> x0, waiting for transfers between devices: 27 us -> none
    another operation x3 -> x0, other arithmetic: 8.48 us -> none
    div x0 -> x3, local copies, waits for them, and re-layouts: none -> 3.47 us  [the longest x2 1.78 us: transforms(): inv = inv / math.sqrt(NFREQ)]
  transfers between devices with their start and end apart: 2 -> 0, of which waited for: 2 -> 0; matrix products, arithmetic and copies ran while one was open for 14% -> 0% of each run, Pallas kernels for 0% -> 0%
where the time goes in v1:
time: 97.6 us; the launch traced here: 97.4 us
  Pallas kernels  86.3 us (88%)
  local copies, waits for them, and re-layouts  7.35 us (8%)
  other arithmetic  3.62 us (4%)
    pallas_call x1, Pallas kernels, apply(): pl.pallas_call(functools.partial(apply_kernel, step), grid=(ROWS,), out_s...  42.5 us
    pallas_call x1, Pallas kernels, spectra(): pl.pallas_call(spectra_kernel, out_shape=jax.ShapeDtypeStruct((EXT, 16, 1...  26.2 us
    pallas_call x1, Pallas kernels, output(): pl.pallas_call(output_kernel, out_shape=jax.ShapeDtypeStruct((16, OUT), B...  17.6 us

profile of v1, /device:TPU:1, one launch (start us, length us, event | category | flops | bytes accessed | tf_op | source)
XLA Modules:
  0.0 97.4 jit_solution(16761069399548005782)
XLA Ops:
  0.0 0.7 dynamic-slice_multiply_fusion
  0.7 0.1 iota_add_fusion
  0.8 0.1 add.46
  0.9 0.8 fusion.3
  1.7 0.3 multiply_multiply_fusion
  2.0 1.7 %div.21 = f32[256,64]{0,1:T(8,128)S(1)} reshape(f32[64,4,8,2,4]{1,0,4,3,2:T(8,128)S(1)} %multiply_multiply_fusion) | data formatting | bytes 131072 | tf_op jit(solution)/shard_map/div | solution.py:291
  3.7 0.1 copy.19
  3.9 0.1 copy.18
  4.0 0.7 pad_maximum_fusion.1.w_ref
  4.7 0.1 copy.15
  4.8 0.0 copy-start
  4.8 0.3 multiply_multiply_fusion.1
  5.1 1.7 %div.18 = f32[64,256]{1,0:T(8,128)S(1)} reshape(f32[8,2,4,64,4]{4,3,2,1,0:T(8,128)S(1)} %multiply_multiply_fusion.1) | data formatting | bytes 131072 | tf_op jit(solution)/shard_map/div | solution.py:289
  6.8 0.6 pad_maximum_fusion.w_ref
  7.5 0.0 copy-done
  7.5 0.6 reshape.180
  8.1 0.3 copy.13
  8.4 0.8 pad.4.t_ref
  9.2 26.2 %shard_map.64.x_ref = f32[70,16,128]{2,1,0:T(8,128)} custom-call(bf16[70,16,128]{2,1,0:T(8,128)(2,1)} %pad.4.t_ref, bf16[128,256]{1,0:T(8,128)(2,1)} %pad_maximum_fusion.w_ref), custom_call_target="tpu_custom_call" | custom-call | tf_op jit(solution)/shard_map/pallas_call | solution.py:108
  35.4 42.5 %shard_map.65.r_ref = f32[12,8,128]{2,1,0:T(8,128)} custom-call(s32[12,1,120]{2,1,0:T(1,128)} %bitcast.21, f32[70,16,128]{2,1,0:T(8,128)} %shard_map.64.x_ref, bf16[12,2,70,32,120]{4,3,2,1,0:T(8,128)(2,1)} %bitcast.17, bf16[12,2,70,32,120]{4,3,2,1,0:T(8,128)(2,1)} %bitcast.18), custom_call_target="tpu_custom_call" | custom-call | tf_op jit(solution)/shard_map/pallas_call | solution.py:198
  77.9 17.6 %shard_map.66 = bf16[16,13440]{1,0:T(8,128)(2,1)} custom-call(f32[12,8,128]{2,1,0:T(8,128)} %shard_map.65.r_ref, bf16[256,128]{1,0:T(8,128)(2,1)} %pad_maximum_fusion.1.w_ref), custom_call_target="tpu_custom_call" | custom-call | tf_op jit(solution)/shard_map/pallas_call | solution.py:265
  95.5 1.9 %reshape.182 = bf16[4,4,13440]{2,1,0:T(4,128)(2,1)} reshape(bf16[16,13440]{1,0:T(8,128)(2,1)} %shard_map.66) | data formatting | bytes 860160 | tf_op jit(solution)/shard_map/reshape | solution.py:303
  (7 shorter events, 0.1 us)
Async XLA Ops:
  4.8 2.7 %copy-start = (bf16[4,4,8400]{2,1,0:T(4,128)(2,1)S(1)}, bf16[4,4,8400]{2,1,0:T(4,128)(2,1)}, u32[]{:S(2)}) copy-start(bf16[4,4,8400]{2,1,0:T(4,128)(2,1)} %param.6) | copy-start | bytes 806404

commit v2 on v1

--- a/solution.py
+++ b/solution.py
@@ -60,7 +60,43 @@
     )
 
 
-def spectra_kernel(t_ref, w_ref, x_ref, a1, s2, b2, s3, b3, own, ss1, rs1, ss2, rs2, ss3, rs3):
+def pick(index, ref, first, count):
+    out = jnp.zeros(index.shape, jnp.int32)
+    for n in range(count):
+        out = jnp.where(index == n, ref[first + n], out)
+    return out
+
+
+def trig(freq, time, part):
+    total = NT * NTILE * NFREQ
+    turn = (freq * time + part * (total // 4)) & (total - 1)
+    return jnp.cos(turn.astype(F32) * (2.0 * math.pi / total))
+
+
+def iota(shape, axis):
+    return lax.broadcasted_iota(jnp.int32, shape, axis)
+
+
+def forward_matrix(freq_ref, slab_ref, g):
+    row, col = iota((64, 1), 0), iota((1, 256), 1)
+    freq = pick(row // 8, freq_ref, 0, NFREQ)
+    time = pick(col // 16, slab_ref, g * NTILE, NTILE) * NT + (col // NV) % NT
+    wave = trig(freq, time, (row // NV) % 2) * (1.0 / math.sqrt(NT * NTILE * NFREQ))
+    hi, lo = split(jnp.where(row % NV == col % NV, wave, 0.0))
+    return jnp.concatenate([hi, lo], axis=0)
+
+
+def inverse_matrix(freq_ref, slab_ref, g):
+    row, col = iota((256, 1), 0), iota((1, 128), 1)
+    freq = pick((col % 64) // 8, freq_ref, 0, NFREQ)
+    time = pick(row // 16, slab_ref, g * NTILE, NTILE) * NT + (row // NV) % NT
+    wave = trig(freq, time, (col // NV) % 2) * (1.0 / math.sqrt(NFREQ))
+    wave = jnp.where(row % NV == col % NV, wave, 0.0)
+    hi = wave.astype(BF16).astype(F32)
+    return jnp.where(col < 64, hi, wave - hi).astype(BF16)
+
+
+def spectra_kernel(freq_ref, slab_ref, t_ref, x_ref, w_ref, a1, s2, b2, s3, b3, own, ss1, rs1, ss2, rs2, ss3, rs3):
     g, k, over_tile, over_freq = peers()
     enter(over_tile, over_freq)
     mine = pltpu.make_async_copy(t_ref.at[pl.ds(chunk_start(k), CHUNK)], a1.at[k], own)
@@ -70,6 +106,7 @@
         c = remote(t_ref.at[pl.ds(chunk_start(kk), CHUNK)], a1.at[k], ss1.at[kk], rs1.at[k], "tile", kk)
         c.start()
         sends.append(c)
+    w_ref[...] = forward_matrix(freq_ref, slab_ref, g)
     mine.wait()
     for _, kk in over_tile:
         remote(t_ref.at[pl.ds(0, CHUNK)], a1.at[kk], ss1.at[kk], rs1.at[kk], "tile", kk).wait_recv()
@@ -102,15 +139,17 @@
         c.wait_send()
 
 
-def spectra(t, w):
+def spectra(freq_bin, slab_order, t):
     vmem = pl.BlockSpec(memory_space=pltpu.VMEM)
+    smem = pl.BlockSpec(memory_space=pltpu.SMEM)
     dma = pltpu.SemaphoreType.DMA
     return pl.pallas_call(
         spectra_kernel,
         out_shape=jax.ShapeDtypeStruct((EXT, 16, 128), F32),
-        in_specs=[vmem, vmem],
+        in_specs=[smem, smem, vmem],
         out_specs=vmem,
         scratch_shapes=[
+            pltpu.VMEM((128, 256), BF16),
             pltpu.VMEM((NTILE, CHUNK, 16, 128), BF16),
             pltpu.VMEM((NFREQ, CHUNK, 8, 128), BF16),
             pltpu.VMEM((NFREQ, CHUNK, 8, 128), BF16),
@@ -120,7 +159,7 @@
             dma((NTILE,)), dma((NTILE,)), dma((NFREQ,)), dma((NFREQ,)), dma((NTILE,)), dma((NTILE,)),
         ],
         compiler_params=pltpu.CompilerParams(collective_id=0, has_side_effects=True),
-    )(t, w)
+    )(freq_bin, slab_order, t)
 
 
 def project(v_ref, x_ref, rank_row, ct):
@@ -153,15 +192,14 @@
 
 
 def expand(u_ref, ct, diag, step):
-    lane = lax.broadcasted_iota(jnp.int32, (step * 16, 128), 1)
     low = lax.broadcasted_iota(jnp.int32, (step, 8, 128), 2) < 64
     for h in range(2):
         @pl.loop(0, EXT // step)
         def _(s):
             us = []
             for c in range(2):
-                u = u_ref[0, c, pl.ds(s * step, step), 16 * h:16 * h + 16, :].reshape(step * 16, 128)
-                us.append(jnp.where(lane < COLS, u, jnp.zeros_like(u)))
+                u = u_ref[0, c, pl.ds(s * step, step), 16 * h:16 * h + 16, :].reshape(step * 16, COLS)
+                us.append(jnp.pad(u, ((0, 0), (0, 128 - COLS))))
             z = lax.dot_general(jnp.concatenate(us, axis=1), ct[h], NT_DIMS, preferred_element_type=F32)
             z = z.reshape(step, 2, 8, 128)
             diag[h, pl.ds(s * step * 8, step * 8), :] = jnp.where(low, z[:, 0], z[:, 1]).reshape(step * 8, 128)
@@ -183,124 +221,112 @@
     return dot(pick, hi) + dot(pick, lo)
 
 
-def apply_kernel(step, rank_ref, x_ref, v_ref, u_ref, out_ref, ct, diag):
-    @pl.when(pl.program_id(0) == 0)
+def apply_kernel(
+    step, freq_ref, slab_ref, rank_ref, x_ref, v_ref, u_ref, out_ref,
+    ct, diag, inv, s1, b1, s2, b2, ss1, rs1, ss2, rs2,
+):
+    i = pl.program_id(0)
+    g, k, over_tile, over_freq = peers()
+    barrier = pltpu.get_barrier_semaphore()
+
+    @pl.when(i == 0)
     def _():
+        for _, kk in over_tile:
+            pl.semaphore_signal(barrier, inc=1, device_id={"tile": kk}, device_id_type=MESH)
+        for _, f in over_freq:
+            pl.semaphore_signal(barrier, inc=1, device_id={"freq": f}, device_id_type=MESH)
         ct[...] = jnp.zeros_like(ct)
+        inv[...] = inverse_matrix(freq_ref, slab_ref, g)
 
     project(v_ref, x_ref, rank_ref[0], ct)
     expand(u_ref, ct, diag, step)
-    out_ref[0] = jnp.zeros((8, 128), F32)
-    out_ref[0, :, 0:EXT] = collect(diag)
-
-
-def apply(ranks, x, v, u, step=14):
+    piece = jnp.pad(collect(diag), ((0, 0), (0, 128 - EXT)))
+    s1[i] = pltpu.roll(piece, lax.rem((k * ROWS + i) * EXT, 128), 1).astype(BF16)
+
+    @pl.when(i == 0)
+    def _():
+        pl.semaphore_wait(barrier, NTILE + NFREQ - 2)
+
+    for _, f in over_freq:
+        remote(s1.at[i], b1.at[i, g], ss1.at[f], rs1.at[i, g], "freq", f).start()
+    b1[i, g] = s1[i]
+
+    def finish(n):
+        for _, f in over_freq:
+            remote(s1.at[n], b1.at[n, f], ss1.at[f], rs1.at[n, f], "freq", f).wait_recv()
+        r = b1[n].reshape(64, 128)
+        res = jnp.dot(inv[...], jnp.concatenate([r, r], axis=0), preferred_element_type=F32)
+        s2[:, n] = res.reshape(NTILE, 16, 128).astype(BF16)
+        for _, kk in over_tile:
+            remote(s2.at[kk, n], b2.at[k, n], ss2.at[kk], rs2.at[k], "tile", kk).start()
+        b2[k, n] = s2[k, n]
+
+    @pl.when(i > 0)
+    def _():
+        finish(i - 1)
+
+    @pl.when(i == ROWS - 1)
+    def _():
+        finish(i)
+        for _, kk in over_tile:
+            remote(s2.at[kk], b2.at[kk], ss2.at[kk], rs2.at[kk], "tile", kk).wait_recv()
+        lane = iota((16, 128), 1)
+        tiles = [[] for _ in range(OUT // 128)]
+        for row in range(NTILE * ROWS):
+            a, off = divmod(row * EXT, 128)
+            val = b2[row // ROWS, row % ROWS]
+            if off + EXT <= 128:
+                tiles[a].append(val)
+            else:
+                tiles[a].append(jnp.where(lane >= off, val, jnp.zeros_like(val)))
+                tiles[a + 1].append(jnp.where(lane < off, val, jnp.zeros_like(val)))
+        for m, vals in enumerate(tiles):
+            out_ref[:, 128 * m:128 * m + 128] = tree(vals)
+        for _, f in over_freq:
+            remote(s1, b1.at[:, f], ss1.at[f], rs1.at[0, f], "freq", f).wait_send()
+        for _, kk in over_tile:
+            remote(s2.at[kk], b2.at[kk], ss2.at[kk], rs2.at[kk], "tile", kk).wait_send()
+
+
+def apply(freq_bin, slab_order, ranks, x, v, u, step=70):
+    dma = pltpu.SemaphoreType.DMA
+    smem = pl.BlockSpec(memory_space=pltpu.SMEM)
+    bases = pl.BlockSpec((1, 2, EXT, RANK, COLS), lambda i: (i, 0, 0, 0, 0))
     return pl.pallas_call(
         functools.partial(apply_kernel, step),
         grid=(ROWS,),
-        out_shape=jax.ShapeDtypeStruct((ROWS, 8, 128), F32),
+        out_shape=jax.ShapeDtypeStruct((16, OUT), BF16),
         in_specs=[
+            smem,
+            smem,
             pl.BlockSpec((1, 1, COLS), lambda i: (i, 0, 0)),
             pl.BlockSpec((EXT, 16, 128), lambda i: (0, 0, 0)),
-            pl.BlockSpec((1, 2, EXT, RANK, COLS), lambda i: (i, 0, 0, 0, 0)),
-            pl.BlockSpec((1, 2, EXT, RANK, 128), lambda i: (i, 0, 0, 0, 0)),
+            bases,
+            bases,
         ],
-        out_specs=pl.BlockSpec((1, 8, 128), lambda i: (i, 0, 0)),
-        scratch_shapes=[pltpu.VMEM((2, 128, 256), BF16), pltpu.VMEM((2, EXT * 8, 128), F32)],
-    )(ranks, x, v, u)
-
-
-def output_kernel(r_ref, w_ref, out_ref, s1, b1, s2, b2, ss1, rs1, ss2, rs2):
-    g, k, over_tile, over_freq = peers()
-    lane = lax.broadcasted_iota(jnp.int32, (8, 128), 1)
-    zero = jnp.zeros((8, 128), F32)
-    tiles = [zero] * 8
-    for i in range(ROWS):
-        a, off = divmod(EXT * i, 128)
-        piece = pltpu.roll(r_ref[i], off, 1) if off else r_ref[i]
-        tiles[a] = tiles[a] + jnp.where(lane >= off, piece, 0.0)
-        if off + EXT > 128:
-            tiles[a + 1] = tiles[a + 1] + jnp.where(lane < off, piece, 0.0)
-    off = lax.rem(k * (EXT * ROWS), 128)
-    rolled = [zero] + [pltpu.roll(t, off, 1) for t in tiles]
-    for a in range(8):
-        s1[:, 128 * a:128 * a + 128] = jnp.where(lane >= off, rolled[a + 1], rolled[a]).astype(BF16)
-    enter(over_tile, over_freq)
-    sends = []
-    for _, f in over_freq:
-        c = remote(s1, b1.at[g], ss1.at[f], rs1.at[g], "freq", f)
-        c.start()
-        sends.append(c)
-    b1[g] = s1[...]
-    for _, f in over_freq:
-        remote(s1, b1.at[f], ss1.at[f], rs1.at[f], "freq", f).wait_recv()
-    r = b1[...].reshape(64, 1024)
-    both = jnp.concatenate([r, r], axis=0)
-    for c in range(4):
-        lanes = slice(256 * c, 256 * c + 256)
-        res = jnp.dot(w_ref[...], both[:, lanes], preferred_element_type=F32)
-        s2[:, :, lanes] = res.reshape(NTILE, 16, 256).astype(BF16)
-    for _, kk in over_tile:
-        c = remote(s2.at[kk], b2.at[k], ss2.at[kk], rs2.at[k], "tile", kk)
-        c.start()
-        sends.append(c)
-    b2[k] = s2[k]
-    for _, kk in over_tile:
-        remote(s2.at[kk], b2.at[kk], ss2.at[kk], rs2.at[kk], "tile", kk).wait_recv()
-    parts = [[] for _ in range(OUT // 128)]
-    for kk in range(NTILE):
-        a, off = divmod(kk * EXT * ROWS, 128)
-        for t in range((off + EXT * ROWS + 127) // 128):
-            parts[a + t].append((kk, t))
-    for m, ps in enumerate(parts):
-        vals = [b2[kk, :, 128 * t:128 * t + 128] for kk, t in ps]
-        out_ref[:, 128 * m:128 * m + 128] = tree(vals)
-    for c in sends:
-        c.wait_send()
-
-
-def output(r, w):
-    vmem = pl.BlockSpec(memory_space=pltpu.VMEM)
-    dma = pltpu.SemaphoreType.DMA
-    return pl.pallas_call(
-        output_kernel,
-        out_shape=jax.ShapeDtypeStruct((16, OUT), BF16),
-        in_specs=[vmem, vmem],
-        out_specs=vmem,
+        out_specs=pl.BlockSpec((16, OUT), lambda i: (0, 0)),
         scratch_shapes=[
-            pltpu.VMEM((8, 1024), BF16),
-            pltpu.VMEM((NFREQ, 8, 1024), BF16),
-            pltpu.VMEM((NTILE, 16, 1024), BF16),
-            pltpu.VMEM((NTILE, 16, 1024), BF16),
-            dma((NFREQ,)), dma((NFREQ,)), dma((NTILE,)), dma((NTILE,)),
+            pltpu.VMEM((2, 128, 256), BF16),
+            pltpu.VMEM((2, EXT * 8, 128), F32),
+            pltpu.VMEM((256, 128), BF16),
+            pltpu.VMEM((ROWS, 8, 128), BF16),
+            pltpu.VMEM((ROWS, NFREQ, 8, 128), BF16),
+            pltpu.VMEM((NTILE, ROWS, 16, 128), BF16),
+            pltpu.VMEM((NTILE, ROWS, 16, 128), BF16),
+            dma((NFREQ,)), dma((ROWS, NFREQ)), dma((NTILE,)), dma((NTILE,)),
         ],
         compiler_params=pltpu.CompilerParams(collective_id=1, has_side_effects=True),
-    )(r, w)
-
-
-def transforms(freq_bin, slab_order):
-    g = lax.axis_index("freq")
-    slabs = lax.dynamic_slice_in_dim(slab_order, g * NTILE, NTILE)
-    times = (slabs[:, None] * NT + jnp.arange(NT, dtype=jnp.int32)[None, :]).reshape(-1)
-    total = NT * NTILE * NFREQ
-    angles = (freq_bin[:, None] * times[None, :] % total).astype(F32) * (2.0 * math.pi / total)
-    trig = jnp.stack([jnp.cos(angles), -jnp.sin(angles)], axis=1)
-    eye = jnp.eye(NV, dtype=F32)
-    fwd = (trig[:, :, None, :, None] * eye[None, None, :, None, :]).reshape(64, 256) / math.sqrt(total)
-    inv = (trig.transpose(2, 0, 1)[:, None, :, :, None] * eye[None, :, None, None, :]).reshape(256, 64)
-    inv = inv / math.sqrt(NFREQ)
-    return jnp.concatenate(split(fwd), axis=0), jnp.concatenate(split(inv), axis=1)
+    )(freq_bin, slab_order, ranks, x, v, u)
 
 
 def local(virtual_source_trace, v_bases, u_bases, ranks, freq_bin, slab_order):
-    fwd, inv = transforms(freq_bin, slab_order)
     t = virtual_source_trace.reshape(NT, NV, COLS, EXT).transpose(3, 0, 1, 2).reshape(EXT, 16, COLS)
     t = jnp.pad(t, ((0, 0), (0, 0), (0, 128 - COLS)))
-    x = spectra(t, fwd)
+    x = spectra(freq_bin, slab_order, t)
     v = v_bases[0].transpose(0, 2, 4, 3, 1)
     u = u_bases[0].transpose(0, 2, 4, 3, 1)
-    r = apply(ranks.reshape(ROWS, 1, COLS), x, v, u)
-    return output(r, inv).reshape(NT, NV, OUT)
+    out = apply(freq_bin, slab_order, ranks.reshape(ROWS, 1, COLS), x, v, u)
+    return out.reshape(NT, NV, OUT)
 
 
 def solution(mesh):

time: 97.6 us -> 78.4 us (0.80)
  Pallas kernels: 86.3 us -> 73.7 us
  other arithmetic: 3.62 us -> 0 us
  local copies, waits for them, and re-layouts: 7.35 us -> 4.51 us
    pallas_call x1 -> x0, Pallas kernels: 17.6 us -> none  [output(): pl.pallas_call(output_kernel, out_shape=jax.ShapeDtypeStruct((16, OUT), B...]
    pallas_call x1, Pallas kernels: 42.5 us -> 47.4 us  [apply(): pl.pallas_call(functools.partial(apply_kernel, step), grid=(ROWS,), out_s...]
    div x3 -> x0, local copies, waits for them, and re-layouts: 3.47 us -> none  [the longest x2 1.78 us: transforms(): inv = inv / math.sqrt(NFREQ)]
    concatenate x2 -> x0, other arithmetic: 1.35 us -> none  [the longest x1 0.72 us: transforms(): jnp.concatenate(split(inv), axis=1)]
where the time goes in v2:
time: 78.4 us; the launch traced here: 78.2 us
  Pallas kernels  73.7 us (94%)
  local copies, waits for them, and re-layouts  4.51 us (6%)
    pallas_call x1, Pallas kernels, apply(): pl.pallas_call(functools.partial(apply_kernel, step), grid=(ROWS,), out_s...  47.4 us
    pallas_call x1, Pallas kernels, spectra(): pl.pallas_call(spectra_kernel, out_shape=jax.ShapeDtypeStruct((EXT, 16, 1...  26.3 us
    reshape x1, local copies, waits for them, and re-layouts, local(): return out.reshape(NT, NV, OUT)  1.87 us

profile of v2, /device:TPU:1, one launch (start us, length us, event | category | flops | bytes accessed | tf_op | source)
XLA Modules:
  0.0 78.2 jit_solution(14473089236510845375)
XLA Ops:
  0.0 1.5 %reshape.13 = bf16[4,4,120,70]{3,2,1,0:T(8,128)(2,1)S(1)} reshape(bf16[4,4,8400]{2,1,0:T(4,128)(2,1)} %param.6) | data formatting | bytes 537600 | tf_op jit(solution)/shard_map/reshape | solution.py:323
  1.5 0.3 copy.8
  1.9 0.8 pad.4.t_ref
  2.7 26.3 %shard_map.64.x_ref = f32[70,16,128]{2,1,0:T(8,128)} custom-call(s32[8]{0:T(128)} %freq_ref.3, s32[128]{0:T(128)} %slab_ref.3, bf16[70,16,128]{2,1,0:T(8,128)(2,1)} %pad.4.t_ref), custom_call_target="tpu_custom_call" | custom-call | tf_op jit(solution)/shard_map/pallas_call | solution.py:146
  29.0 47.4 %shard_map.65 = bf16[16,13440]{1,0:T(8,128)(2,1)} custom-call(s32[8]{0:T(128)} %freq_ref.3, s32[128]{0:T(128)} %slab_ref.3, s32[12,1,120]{2,1,0:T(1,128)} %bitcast.13, f32[70,16,128]{2,1,0:T(8,128)} %shard_map.64.x_ref, bf16[12,2,70,32,120]{4,3,2,1,0:T(8,128)(2,1)} %bitcast.9, bf16[12,2,70,32,120]{4,3,2,1,0:T(8,128)(2,1)} %bitcast.10), custom_call_target="tpu_custom_call" | custom-call | tf_op jit(solution)/shard_map/pallas_call | solution.py:295
  76.3 1.9 %reshape.15 = bf16[4,4,13440]{2,1,0:T(4,128)(2,1)} reshape(bf16[16,13440]{1,0:T(8,128)(2,1)} %shard_map.65) | data formatting | bytes 860160 | tf_op jit(solution)/shard_map/reshape | solution.py:329

commit v3 on v2

v3 whole, which is shorter than its diff:
```python
import functools
import math

import jax
import jax.numpy as jnp
from jax import lax
from jax.experimental import pallas as pl
from jax.experimental.pallas import tpu as pltpu
from jax.sharding import PartitionSpec as P

F32, BF16 = jnp.float32, jnp.bfloat16
MESH = pl.DeviceIdType.MESH
EXT = 70
COLS = 120
RANK = 32
NV = 4
NT = 4
ROWS = 12
NTILE = 16
NFREQ = 8
CHUNK = 5
PARTS = ((0, 5),)
BATCH = 3
NB = ROWS // BATCH
OUT = 13440
NT_DIMS = (((1,), (1,)), ((), ()))


def chunk_start(k):
    return (k * (EXT - CHUNK) + 7) // (NTILE - 1)


def split(x):
    hi = x.astype(BF16)
    return hi, (x - hi.astype(F32)).astype(BF16)


def tree(xs):
    while len(xs) > 1:
        xs = [a + b for a, b in zip(xs[::2], xs[1::2])] + ([xs[-1]] if len(xs) % 2 else [])
    return xs[0]


def peers():
    g, k = lax.axis_index("freq"), lax.axis_index("tile")
    over_tile = [(d, lax.rem(k + d, NTILE)) for d in range(1, NTILE)]
    over_freq = [(d, lax.rem(g + d, NFREQ)) for d in range(1, NFREQ)]
    return g, k, over_tile, over_freq


def remote(src, dst, send, recv, axis, to):
    return pltpu.make_async_remote_copy(
        src_ref=src, dst_ref=dst, send_sem=send, recv_sem=recv, device_id={axis: to}, device_id_type=MESH
    )


def pick(index, ref, first, count):
    out = jnp.zeros(index.shape, jnp.int32)
    for n in range(count):
        out = jnp.where(index == n, ref[first + n], out)
    return out


def trig(freq, time, part):
    total = NT * NTILE * NFREQ
    turn = (freq * time + part * (total // 4)) & (total - 1)
    return jnp.cos(turn.astype(F32) * (2.0 * math.pi / total))


def iota(shape, axis):
    return lax.broadcasted_iota(jnp.int32, shape, axis)


def forward_matrix(freq_ref, slab_ref, g):
    row, col = iota((64, 1), 0), iota((1, 256), 1)
    freq = pick(row // 8, freq_ref, 0, NFREQ)
    time = pick(col // 16, slab_ref, g * NTILE, NTILE) * NT + (col // NV) % NT
    wave = trig(freq, time, (row // NV) % 2) * (1.0 / math.sqrt(NT * NTILE * NFREQ))
    hi, lo = split(jnp.where(row % NV == col % NV, wave, 0.0))
    return jnp.concatenate([hi, lo], axis=0)


def inverse_matrix(freq_ref, slab_ref, g):
    row, col = iota((256, 1), 0), iota((1, 128), 1)
    freq = pick((col % 64) // 8, freq_ref, 0, NFREQ)
    time = pick(row // 16, slab_ref, g * NTILE, NTILE) * NT + (row // NV) % NT
    wave = trig(freq, time, (col // NV) % 2) * (1.0 / math.sqrt(NFREQ))
    wave = jnp.where(row % NV == col % NV, wave, 0.0)
    hi = wave.astype(BF16).astype(F32)
    return jnp.where(col < 64, hi, wave - hi).astype(BF16)


def spectra(g, k, over_tile, over_freq, mats, t_ref, x_ref, w_ref, a1, s2, b2, s3, b3, own, ss1, rs1, ss2, rs2, ss3, rs3):
    mine = pltpu.make_async_copy(t_ref.at[pl.ds(chunk_start(k), CHUNK)], a1.at[k], own)
    mine.start()
    sends = []
    for n, (o, size) in enumerate(PARTS):
        for _, kk in over_tile:
            c = remote(
                t_ref.at[pl.ds(chunk_start(kk) + o, size)], a1.at[k, o:o + size], ss1.at[n, kk], rs1.at[n, k], "tile", kk
            )
            c.start()
            sends.append(c)
    mats()
    mine.wait()
    for n, (o, size) in enumerate(PARTS):
        for _, kk in over_tile:
            dst = a1.at[kk, o:o + size]
            remote(dst, dst, ss1.at[n, kk], rs1.at[n, kk], "tile", kk).wait_recv()
        for p in range(o, o + size):
            data = a1[:, p].reshape(NTILE * 16, COLS)
            both = jnp.dot(w_ref[...], data, preferred_element_type=F32)
            s2[:, p] = (both[:64] + both[64:]).reshape(NFREQ, 8, COLS).astype(BF16)
        for _, f in over_freq:
            c = remote(s2.at[f, o:o + size], b2.at[g, o:o + size], ss2.at[n, f], rs2.at[n, g], "freq", f)
            c.start()
            sends.append(c)
    for n, (o, size) in enumerate(PARTS):
        total = s2[g, o:o + size].astype(F32)
        for _, f in over_freq:
            dst = b2.at[f, o:o + size]
            remote(dst, dst, ss2.at[n, f], rs2.at[n, f], "freq", f).wait_recv()
            total = total + b2[f, o:o + size].astype(F32)
        s3[o:o + size] = total.astype(BF16)
        for _, kk in over_tile:
            c = remote(s3.at[o:o + size], b3.at[k, o:o + size], ss3.at[n, kk], rs3.at[n, k], "tile", kk)
            c.start()
            sends.append(c)
    b3[k] = s3[...]
    for n, (o, size) in enumerate(PARTS):
        for _, kk in over_tile:
            dst = b3.at[kk, o:o + size]
            remote(dst, dst, ss3.at[n, kk], rs3.at[n, kk], "tile", kk).wait_recv()
    for kk in range(NTILE):
        for p in range(CHUNK):
            x = b3[kk, p].astype(F32)
            xr, xi = x[0:4], x[4:8]
            x_ref[chunk_start(kk) + p] = jnp.concatenate([xr, xi - xr, xr + xi, xr], axis=0)
    for c in sends:
        c.wait_send()


def project(v_ref, x_ref, rank_row, ct):
    row = lax.broadcasted_iota(jnp.int32, (8, COLS), 0)
    for h in range(2):
        def body(p, acc):
            acc = list(acc)
            for a in range(2):
                r = 16 * h + 8 * a
                re = v_ref[0, p, r:r + 8, :].astype(F32)
                im = v_ref[1, p, r:r + 8, :].astype(F32)
                for n, b in enumerate((re + im, re, im)):
                    for v in range(NV):
                        m = 4 * n + v
                        acc[12 * a + m] += b * jnp.broadcast_to(x_ref[p, m:m + 1, :COLS], (8, COLS))
            return tuple(acc)

        acc = lax.fori_loop(0, EXT, body, (jnp.zeros((8, COLS), F32),) * 24, unroll=5)
        for a in range(2):
            keep = row + (16 * h + 8 * a) < rank_row
            for v in range(NV):
                k1, k2, k3 = (acc[12 * a + 4 * n + v] for n in range(3))
                re = jnp.where(keep, k1 - k3, 0.0).astype(BF16)
                im = jnp.where(keep, k1 + k2, 0.0).astype(BF16)
                n = 128 * h + 64 * a + 16 * v
                ct[n:n + 8, 0:COLS] = re
                ct[n:n + 8, 128:128 + COLS] = -im
                ct[n + 8:n + 16, 0:COLS] = im
                ct[n + 8:n + 16, 128:128 + COLS] = re


def expand(u_ref, ct, diag):
    low = iota((EXT, 8, 128), 2) < 64
    us = [jnp.pad(u_ref[c].reshape(EXT * RANK, COLS), ((0, 0), (0, 128 - COLS))) for c in range(2)]
    z = lax.dot_general(jnp.concatenate(us, axis=1), ct[...], NT_DIMS, preferred_element_type=F32)
    z = z.reshape(EXT, 4, 8, 256)
    for h in range(2):
        lanes = slice(128 * h, 128 * h + 128)
        diag[h] = jnp.where(low, z[:, 2 * h, :, lanes], z[:, 2 * h + 1, :, lanes]).reshape(EXT * 8, 128)


def collect(diag):
    lane = lax.broadcasted_iota(jnp.int32, (EXT, 128), 1) % 8
    halves = []
    for h in range(2):
        tot = diag[h, pl.ds(0, EXT, stride=8), :]
        for b in range(1, 8):
            tot = jnp.where(lane == b, diag[h, pl.ds(b, EXT, stride=8), :], tot)
        halves.append(tot)
    hi, lo = split(jnp.concatenate(halves, axis=1))
    rows = lax.broadcasted_iota(jnp.int32, (8, 256), 0)
    lanes = lax.broadcasted_iota(jnp.int32, (8, 256), 1)
    pick = ((lanes % 64) // 8 == (rows % 4) * 2 + rows // 4).astype(BF16)
    dot = functools.partial(lax.dot_general, dimension_numbers=NT_DIMS, preferred_element_type=F32)
    return dot(pick, hi) + dot(pick, lo)


def apply_kernel(
    freq_ref, slab_ref, t_ref, rank_ref, v_hbm, u_hbm, b2,
    v_all, u_all, x_ref, w_ref, ct, diag, inv, ring, s1, b1, s2, vs, us, ss1, rs1, ss2, rs2, own, *scratch
):
    i = pl.program_id(0)
    g, k, over_tile, over_freq = peers()
    barrier = pltpu.get_barrier_semaphore()

    @pl.when(i == 0)
    def _():
        for _, kk in over_tile:
            pl.semaphore_signal(barrier, inc=1, device_id={"tile": kk}, device_id_type=MESH)
        for _, f in over_freq:
            pl.semaphore_signal(barrier, inc=1, device_id={"freq": f}, device_id_type=MESH)
        for n in range(ROWS):
            pltpu.make_async_copy(v_hbm.at[n], v_all.at[n], vs.at[n]).start()
            pltpu.make_async_copy(u_hbm.at[n], u_all.at[n], us.at[n]).start()
        ct[...] = jnp.zeros_like(ct)

        def mats():
            w_ref[...] = forward_matrix(freq_ref, slab_ref, g)
            inv[...] = inverse_matrix(freq_ref, slab_ref, g)

        pl.semaphore_wait(barrier, NTILE + NFREQ - 2)
        spectra(g, k, over_tile, over_freq, mats, t_ref, x_ref, w_ref, *scratch)

    pltpu.make_async_copy(v_hbm.at[i], v_all.at[i], vs.at[i]).wait()
    project(v_all.at[i], x_ref, rank_ref[i], ct)
    pltpu.make_async_copy(u_hbm.at[i], u_all.at[i], us.at[i]).wait()
    expand(u_all.at[i], ct, diag)
    piece = jnp.pad(collect(diag), ((0, 0), (0, 128 - EXT)))
    batch, turn = lax.div(i, BATCH), lax.rem(i, BATCH)
    start = (k * ROWS + i) * EXT
    off = lax.rem(start, 128)
    piece = pltpu.roll(piece, off, 1)
    head = iota((8, 128), 1) >= off
    odd = lax.rem(lax.div(start, 128), 2) == 1
    for t in range(2):
        before = jnp.where(turn == 0, 0.0, ring[t])
        ring[t] = before + jnp.where(head == (odd if t else jnp.logical_not(odd)), piece, 0.0)

    def finish(n):
        for _, f in over_freq:
            remote(s1.at[n], b1.at[n, f], ss1.at[f], rs1.at[n, f], "freq", f).wait_recv()
        r = b1[n].reshape(64, 256)
        res = jnp.dot(inv[...], jnp.concatenate([r, r], axis=0), preferred_element_type=F32)
        s2[:, n] = res.reshape(NTILE, 16, 256).astype(BF16)
        for _, kk in over_tile:
            remote(s2.at[kk, n], b2.at[k, n], ss2.at[kk], rs2.at[k], "tile", kk).start()
        pltpu.make_async_copy(s2.at[k, n], b2.at[k, n], own.at[n]).start()

    @pl.when(jnp.logical_and(turn == 0, i > 0))
    def _():
        finish(batch - 1)

    @pl.when(turn == BATCH - 1)
    def _():
        s1[batch] = jnp.concatenate([ring[0], ring[1]], axis=1).astype(BF16)
        for _, f in over_freq:
            remote(s1.at[batch], b1.at[batch, g], ss1.at[f], rs1.at[batch, g], "freq", f).start()
        b1[batch, g] = s1[batch]

    @pl.when(i == ROWS - 1)
    def _():
        finish(NB - 1)
        for _, kk in over_tile:
            remote(s2.at[kk], b2.at[kk], ss2.at[kk], rs2.at[kk], "tile", kk).wait_recv()
        for n in range(NB):
            pltpu.make_async_copy(s2.at[k, n], b2.at[k, n], own.at[n]).wait()
        for _, f in over_freq:
            remote(s1, b1.at[:, f], ss1.at[f], rs1.at[0, f], "freq", f).wait_send()
        for _, kk in over_tile:
            remote(s2.at[kk], b2.at[kk], ss2.at[kk], rs2.at[kk], "tile", kk).wait_send()


def apply(freq_bin, slab_order, t, ranks, v, u):
    dma = pltpu.SemaphoreType.DMA
    smem = pl.BlockSpec(memory_space=pltpu.SMEM)
    vmem = pl.BlockSpec(memory_space=pltpu.VMEM)
    hbm = pl.BlockSpec(memory_space=pl.ANY)
    return pl.pallas_call(
        apply_kernel,
        grid=(ROWS,),
        out_shape=jax.ShapeDtypeStruct((NTILE, NB, 16, 256), BF16),
        in_specs=[smem, smem, vmem, vmem, hbm, hbm],
        out_specs=hbm,
        scratch_shapes=[
            pltpu.VMEM((ROWS, 2, EXT, RANK, COLS), BF16),
            pltpu.VMEM((ROWS, 2, EXT, RANK, COLS), BF16),
            pltpu.VMEM((EXT, 16, COLS), F32),
            pltpu.VMEM((128, 256), BF16),
            pltpu.VMEM((256, 256), BF16),
            pltpu.VMEM((2, EXT * 8, 128), F32),
            pltpu.VMEM((256, 128), BF16),
            pltpu.VMEM((2, 8, 128), F32),
            pltpu.VMEM((NB, 8, 256), BF16),
            pltpu.VMEM((NB, NFREQ, 8, 256), BF16),
            pltpu.VMEM((NTILE, NB, 16, 256), BF16),
            dma((ROWS,)), dma((ROWS,)),
            dma((NFREQ,)), dma((NB, NFREQ)), dma((NTILE,)), dma((NTILE,)), dma((NB,)),
            pltpu.VMEM((NTILE, CHUNK, 16, COLS), BF16),
            pltpu.VMEM((NFREQ, CHUNK, 8, COLS), BF16),
            pltpu.VMEM((NFREQ, CHUNK, 8, COLS), BF16),
            pltpu.VMEM((CHUNK, 8, COLS), BF16),
            pltpu.VMEM((NTILE, CHUNK, 8, COLS), BF16),
            dma,
            *(dma((len(PARTS), n)) for n in (NTILE, NTILE, NFREQ, NFREQ, NTILE, NTILE)),
        ],
        compiler_params=pltpu.CompilerParams(collective_id=0, has_side_effects=True),
    )(freq_bin, slab_order, t, ranks, v, u)


def assemble_kernel(b_ref, out_ref):
    lane = iota((16, 128), 1)
    width = BATCH * EXT
    for m in range(OUT // 128):
        vals = []
        for row in range(128 * m // width, (128 * m + 127) // width + 1):
            val = b_ref[row // NB, row % NB, :, 128 * (m % 2):128 * (m % 2) + 128]
            lo, hi = row * width - 128 * m, (row + 1) * width - 128 * m
            if lo > 0:
                val = jnp.where(lane >= lo, val, jnp.zeros_like(val))
            if hi < 128:
                val = jnp.where(lane < hi, val, jnp.zeros_like(val))
            vals.append(val)
        val = tree(vals)
        for t in range(NT):
            out_ref[t, m] = val[NV * t:NV * t + NV]


def assemble(b):
    vmem = pl.BlockSpec(memory_space=pltpu.VMEM)
    return pl.pallas_call(
        assemble_kernel,
        out_shape=jax.ShapeDtypeStruct((NT, OUT // 128, NV, 128), BF16),
        in_specs=[vmem],
        out_specs=vmem,
    )(b)


def local(virtual_source_trace, v_bases, u_bases, ranks, freq_bin, slab_order):
    t = virtual_source_trace.reshape(NT, NV, COLS, EXT).transpose(3, 0, 1, 2).reshape(EXT, 16, COLS)
    v = v_bases[0].transpose(0, 2, 4, 3, 1)
    u = u_bases[0].transpose(0, 2, 4, 3, 1)
    out = assemble(apply(freq_bin, slab_order, t, ranks.reshape(ROWS, 1, COLS), v, u))
    return out.transpose(0, 2, 1, 3).reshape(NT, NV, OUT)


def solution(mesh):
    in_specs = (
        P(("freq", "tile"), None, None),
        P("freq", "tile", None, None, None, None),
        P("freq", "tile", None, None, None, None),
        P("freq", "tile", None),
        P(),
        P(),
    )
    out_specs = P(("freq", "tile"), None, None)
    return jax.shard_map(local, mesh=mesh, in_specs=in_specs, out_specs=out_specs, check_vma=False)
```

time: 78.4 us -> 69.9 us (0.89)
  Pallas kernels: 73.7 us -> 67.2 us
  local copies, waits for them, and re-layouts: 4.51 us -> 2.57 us
    pallas_call x2, Pallas kernels: 73.7 us -> 67.2 us  [the longest x1 65.2 us: apply(): pl.pallas_call(apply_kernel, grid=(ROWS,), out_shape=jax.ShapeDtypeStruct...]
    reshape x1 -> x0, local copies, waits for them, and re-layouts: 1.87 us -> none  [local(): return out.reshape(NT, NV, OUT)]
where the time goes in v3:
time: 69.9 us; the launch traced here: 69.7 us
  Pallas kernels  67.2 us (96%)
  local copies, waits for them, and re-layouts  2.57 us (4%)
    pallas_call x1, Pallas kernels, apply(): pl.pallas_call(apply_kernel, grid=(ROWS,), out_shape=jax.ShapeDtypeStruct...  65.2 us
    pallas_call x1, Pallas kernels, assemble(): pl.pallas_call(assemble_kernel, out_shape=jax.ShapeDtypeStruct((NT, OUT /...  1.96 us
    reshape x1, local copies, waits for them, and re-layouts, local(): virtual_source_trace.reshape(NT, NV, COLS, EXT).transpose(3, 0, 1, 2)  1.54 us

profile of v3, /device:TPU:1, one launch (start us, length us, event | category | flops | bytes accessed | tf_op | source)
XLA Modules:
  0.0 69.7 jit_solution(15839043100079982580)
XLA Ops:
  0.0 1.5 %reshape.12 = bf16[4,4,120,70]{3,2,1,0:T(8,128)(2,1)S(1)} reshape(bf16[4,4,8400]{2,1,0:T(4,128)(2,1)} %param.6) | data formatting | bytes 537600 | tf_op jit(solution)/shard_map/reshape | solution.py:339
  1.5 1.0 %copy.8 = bf16[70,4,4,120]{3,2,1,0:T(4,128)(2,1)} copy(bf16[70,4,4,120]{0,3,2,1:T(8,128)(2,1)S(1)} %bitcast.14) | data formatting | bytes 537600 | tf_op jit(solution)/shard_map/transpose | solution.py:339
  2.6 65.2 %shard_map.64.b_ref = bf16[16,4,16,256]{3,2,1,0:T(8,128)(2,1)} custom-call(s32[8]{0:T(128)} %freq_ref.1, s32[128]{0:T(128)} %slab_ref.1, bf16[70,16,120]{2,1,0:T(8,128)(2,1)} %bitcast.15, s32[12,1,120]{2,1,0:T(1,128)} %bitcast.16, bf16[12,2,70,32,120]{4,3,2,1,0:T(8,128)(2,1)} %bitcast.12, bf16[12,2,70,32,120]{4,3,2,1,0:T(8,128)(2,1)} %bitcast.13), custom_call_target="tpu_custom_call" | custom-call | tf_op jit(solution)/shard_map/pallas_call | solution.py:278
  67.8 2.0 %shard_map.65 = bf16[4,105,4,128]{3,2,1,0:T(4,128)(2,1)} custom-call(bf16[16,4,16,256]{3,2,1,0:T(8,128)(2,1)} %shard_map.64.b_ref), custom_call_target="tpu_custom_call" | custom-call | tf_op jit(solution)/shard_map/pallas_call | solution.py:330

commit v4 on v3

--- a/solution.py
+++ b/solution.py
@@ -155,7 +155,7 @@
                         acc[12 * a + m] += b * jnp.broadcast_to(x_ref[p, m:m + 1, :COLS], (8, COLS))
             return tuple(acc)
 
-        acc = lax.fori_loop(0, EXT, body, (jnp.zeros((8, COLS), F32),) * 24, unroll=5)
+        acc = lax.fori_loop(0, EXT, body, (jnp.zeros((8, COLS), F32),) * 24, unroll=35)
         for a in range(2):
             keep = row + (16 * h + 8 * a) < rank_row
             for v in range(NV):
@@ -213,6 +213,7 @@
             pltpu.make_async_copy(v_hbm.at[n], v_all.at[n], vs.at[n]).start()
             pltpu.make_async_copy(u_hbm.at[n], u_all.at[n], us.at[n]).start()
         ct[...] = jnp.zeros_like(ct)
+        diag[...] = jnp.zeros_like(diag)
 
         def mats():
             w_ref[...] = forward_matrix(freq_ref, slab_ref, g)
@@ -224,17 +225,22 @@
     pltpu.make_async_copy(v_hbm.at[i], v_all.at[i], vs.at[i]).wait()
     project(v_all.at[i], x_ref, rank_ref[i], ct)
     pltpu.make_async_copy(u_hbm.at[i], u_all.at[i], us.at[i]).wait()
-    expand(u_all.at[i], ct, diag)
-    piece = jnp.pad(collect(diag), ((0, 0), (0, 128 - EXT)))
-    batch, turn = lax.div(i, BATCH), lax.rem(i, BATCH)
-    start = (k * ROWS + i) * EXT
-    off = lax.rem(start, 128)
-    piece = pltpu.roll(piece, off, 1)
-    head = iota((8, 128), 1) >= off
-    odd = lax.rem(lax.div(start, 128), 2) == 1
-    for t in range(2):
-        before = jnp.where(turn == 0, 0.0, ring[t])
-        ring[t] = before + jnp.where(head == (odd if t else jnp.logical_not(odd)), piece, 0.0)
+
+    def place(n, piece):
+        start = (k * ROWS + n) * EXT
+        off = lax.rem(start, 128)
+        piece = pltpu.roll(jnp.pad(piece, ((0, 0), (0, 128 - EXT))), off, 1)
+        head = iota((8, 128), 1) >= off
+        odd = lax.rem(lax.div(start, 128), 2) == 1
+        for t in range(2):
+            before = jnp.where(lax.rem(n, BATCH) == 0, 0.0, ring[t])
+            ring[t] = before + jnp.where(head == (odd if t else jnp.logical_not(odd)), piece, 0.0)
+
+    def send(n):
+        s1[n] = jnp.concatenate([ring[0], ring[1]], axis=1).astype(BF16)
+        for _, f in over_freq:
+            remote(s1.at[n], b1.at[n, g], ss1.at[f], rs1.at[n, g], "freq", f).start()
+        b1[n, g] = s1[n]
 
     def finish(n):
         for _, f in over_freq:
@@ -246,19 +252,22 @@
             remote(s2.at[kk, n], b2.at[k, n], ss2.at[kk], rs2.at[k], "tile", kk).start()
         pltpu.make_async_copy(s2.at[k, n], b2.at[k, n], own.at[n]).start()
 
-    @pl.when(jnp.logical_and(turn == 0, i > 0))
+    last = collect(diag)
+    expand(u_all.at[i], ct, diag)
+    place(jnp.maximum(i - 1, 0), last)
+
+    @pl.when(jnp.logical_and(lax.rem(i, BATCH) == 0, i > 0))
     def _():
-        finish(batch - 1)
-
-    @pl.when(turn == BATCH - 1)
+        send(lax.div(i, BATCH) - 1)
+
+    @pl.when(jnp.logical_and(lax.rem(i, BATCH) == 1, i > BATCH))
     def _():
-        s1[batch] = jnp.concatenate([ring[0], ring[1]], axis=1).astype(BF16)
-        for _, f in over_freq:
-            remote(s1.at[batch], b1.at[batch, g], ss1.at[f], rs1.at[batch, g], "freq", f).start()
-        b1[batch, g] = s1[batch]
+        finish(lax.div(i, BATCH) - 1)
 
     @pl.when(i == ROWS - 1)
     def _():
+        place(i, collect(diag))
+        send(NB - 1)
         finish(NB - 1)
         for _, kk in over_tile:
             remote(s2.at[kk], b2.at[kk], ss2.at[kk], rs2.at[kk], "tile", kk).wait_recv()

time: 69.9 us -> 66.9 us (0.957)
  Pallas kernels: 67.2 us -> 64.1 us
    pallas_call x1, Pallas kernels: 65.2 us -> 62.1 us  [apply(): pl.pallas_call(apply_kernel, grid=(ROWS,), out_shape=jax.ShapeDtypeStruct...]
where the time goes in v4:
time: 66.9 us; the launch traced here: 66.7 us
  Pallas kernels  64.1 us (96%)
  local copies, waits for them, and re-layouts  2.57 us (4%)
    pallas_call x1, Pallas kernels, apply(): pl.pallas_call(apply_kernel, grid=(ROWS,), out_shape=jax.ShapeDtypeStruct...  62.1 us
    pallas_call x1, Pallas kernels, assemble(): pl.pallas_call(assemble_kernel, out_shape=jax.ShapeDtypeStruct((NT, OUT /...  1.96 us
    reshape x1, local copies, waits for them, and re-layouts, local(): virtual_source_trace.reshape(NT, NV, COLS, EXT).transpose(3, 0, 1, 2)  1.54 us

profile of v4, /device:TPU:1, one launch (start us, length us, event | category | flops | bytes accessed | tf_op | source)
XLA Modules:
  0.0 66.7 jit_solution(9411867655779322445)
XLA Ops:
  0.0 1.5 %reshape.12 = bf16[4,4,120,70]{3,2,1,0:T(8,128)(2,1)S(1)} reshape(bf16[4,4,8400]{2,1,0:T(4,128)(2,1)} %param.6) | data formatting | bytes 537600 | tf_op jit(solution)/shard_map/reshape | solution.py:348
  1.5 1.0 %copy.8 = bf16[70,4,4,120]{3,2,1,0:T(4,128)(2,1)} copy(bf16[70,4,4,120]{0,3,2,1:T(8,128)(2,1)S(1)} %bitcast.14) | data formatting | bytes 537600 | tf_op jit(solution)/shard_map/transpose | solution.py:348
  2.6 62.1 %shard_map.64.b_ref = bf16[16,4,16,256]{3,2,1,0:T(8,128)(2,1)} custom-call(s32[8]{0:T(128)} %freq_ref.1, s32[128]{0:T(128)} %slab_ref.1, bf16[70,16,120]{2,1,0:T(8,128)(2,1)} %bitcast.15, s32[12,1,120]{2,1,0:T(1,128)} %bitcast.16, bf16[12,2,70,32,120]{4,3,2,1,0:T(8,128)(2,1)} %bitcast.12, bf16[12,2,70,32,120]{4,3,2,1,0:T(8,128)(2,1)} %bitcast.13), custom_call_target="tpu_custom_call" | custom-call | tf_op jit(solution)/shard_map/pallas_call | solution.py:287
  64.7 2.0 %shard_map.65 = bf16[4,105,4,128]{3,2,1,0:T(4,128)(2,1)} custom-call(bf16[16,4,16,256]{3,2,1,0:T(8,128)(2,1)} %shard_map.64.b_ref), custom_call_target="tpu_custom_call" | custom-call | tf_op jit(solution)/shard_map/pallas_call | solution.py:339

commit v5 on v4

--- a/solution.py
+++ b/solution.py
@@ -43,8 +43,11 @@
 
 def peers():
     g, k = lax.axis_index("freq"), lax.axis_index("tile")
-    over_tile = [(d, lax.rem(k + d, NTILE)) for d in range(1, NTILE)]
-    over_freq = [(d, lax.rem(g + d, NFREQ)) for d in range(1, NFREQ)]
+    far = (0, 1, 2, 1)
+    steps = sorted(range(1, NTILE), key=lambda d: -far[d // 4] - far[d % 4])
+    over_tile = [(d, lax.rem(k // 4 + d // 4, 4) * 4 + lax.rem(k % 4 + d % 4, 4)) for d in steps]
+    steps = sorted(range(1, NFREQ), key=lambda d: -far[d // 2])
+    over_freq = [(d, lax.rem(g // 2 + d // 2, 4) * 2 + lax.rem(g % 2 + d % 2, 2)) for d in steps]
     return g, k, over_tile, over_freq
 
 
@@ -127,15 +130,19 @@
             c.start()
             sends.append(c)
     b3[k] = s3[...]
-    for n, (o, size) in enumerate(PARTS):
-        for _, kk in over_tile:
-            dst = b3.at[kk, o:o + size]
-            remote(dst, dst, ss3.at[n, kk], rs3.at[n, kk], "tile", kk).wait_recv()
-    for kk in range(NTILE):
+
+    def table(kk):
         for p in range(CHUNK):
             x = b3[kk, p].astype(F32)
             xr, xi = x[0:4], x[4:8]
             x_ref[chunk_start(kk) + p] = jnp.concatenate([xr, xi - xr, xr + xi, xr], axis=0)
+
+    table(k)
+    for _, kk in over_tile[::-1]:
+        for n, (o, size) in enumerate(PARTS):
+            dst = b3.at[kk, o:o + size]
+            remote(dst, dst, ss3.at[n, kk], rs3.at[n, kk], "tile", kk).wait_recv()
+        table(kk)
     for c in sends:
         c.wait_send()
 
@@ -260,14 +267,15 @@
     def _():
         send(lax.div(i, BATCH) - 1)
 
-    @pl.when(jnp.logical_and(lax.rem(i, BATCH) == 1, i > BATCH))
+    @pl.when(jnp.logical_and(lax.rem(i, BATCH) == 0, i > BATCH))
     def _():
-        finish(lax.div(i, BATCH) - 1)
+        finish(lax.div(i, BATCH) - 2)
 
     @pl.when(i == ROWS - 1)
     def _():
         place(i, collect(diag))
         send(NB - 1)
+        finish(NB - 2)
         finish(NB - 1)
         for _, kk in over_tile:
             remote(s2.at[kk], b2.at[kk], ss2.at[kk], rs2.at[kk], "tile", kk).wait_recv()

time: 66.9 us -> 60.2 us (0.90)
  Pallas kernels: 64.1 us -> 57.5 us
    pallas_call x1, Pallas kernels: 62.1 us -> 55.5 us  [apply(): pl.pallas_call(apply_kernel, grid=(ROWS,), out_shape=jax.ShapeDtypeStruct...]
where the time goes in v5:
time: 60.2 us; the launch traced here: 60 us
  Pallas kernels  57.5 us (96%)
  local copies, waits for them, and re-layouts  2.57 us (4%)
    pallas_call x1, Pallas kernels, apply(): pl.pallas_call(apply_kernel, grid=(ROWS,), out_shape=jax.ShapeDtypeStruct...  55.5 us
    pallas_call x1, Pallas kernels, assemble(): pl.pallas_call(assemble_kernel, out_shape=jax.ShapeDtypeStruct((NT, OUT /...  1.96 us
    reshape x1, local copies, waits for them, and re-layouts, local(): virtual_source_trace.reshape(NT, NV, COLS, EXT).transpose(3, 0, 1, 2)  1.54 us

profile of v5, /device:TPU:1, one launch (start us, length us, event | category | flops | bytes accessed | tf_op | source)
XLA Modules:
  0.0 60.0 jit_solution(1044890406480930763)
XLA Ops:
  0.0 1.5 %reshape.12 = bf16[4,4,120,70]{3,2,1,0:T(8,128)(2,1)S(1)} reshape(bf16[4,4,8400]{2,1,0:T(4,128)(2,1)} %param.6) | data formatting | bytes 537600 | tf_op jit(solution)/shard_map/reshape | solution.py:356
  1.5 1.0 %copy.8 = bf16[70,4,4,120]{3,2,1,0:T(4,128)(2,1)} copy(bf16[70,4,4,120]{0,3,2,1:T(8,128)(2,1)S(1)} %bitcast.14) | data formatting | bytes 537600 | tf_op jit(solution)/shard_map/transpose | solution.py:356
  2.6 55.5 %shard_map.64.b_ref = bf16[16,4,16,256]{3,2,1,0:T(8,128)(2,1)} custom-call(s32[8]{0:T(128)} %freq_ref.1, s32[128]{0:T(128)} %slab_ref.1, bf16[70,16,120]{2,1,0:T(8,128)(2,1)} %bitcast.15, s32[12,1,120]{2,1,0:T(1,128)} %bitcast.16, bf16[12,2,70,32,120]{4,3,2,1,0:T(8,128)(2,1)} %bitcast.12, bf16[12,2,70,32,120]{4,3,2,1,0:T(8,128)(2,1)} %bitcast.13), custom_call_target="tpu_custom_call" | custom-call | tf_op jit(solution)/shard_map/pallas_call | solution.py:295
  58.1 2.0 %shard_map.65 = bf16[4,105,4,128]{3,2,1,0:T(4,128)(2,1)} custom-call(bf16[16,4,16,256]{3,2,1,0:T(8,128)(2,1)} %shard_map.64.b_ref), custom_call_target="tpu_custom_call" | custom-call | tf_op jit(solution)/shard_map/pallas_call | solution.py:347
